TPU v7x, 32 devices: a whole 2x2x4 slice. The times are simulated.
32 devices in a mesh: wide: 16 (over z, x, core), narrow: 2 (over y).
Axes of the slice: x: 2, y: 2, z: 4, core: 2. Of those that a mesh axis runs over, the one named last changes fastest.
Arguments:
- tokens_short: bfloat16 [32, 128, 768], P(('wide', 'narrow')), may hold values from -6 to 6
- tokens_long: bfloat16 [32, 512, 768], P(('wide', 'narrow')), may hold values from -6 to 6
- in_weight: bfloat16 [768, 2304], P('wide', 'narrow'), may hold values from -0.21875 to 0.21875
- in_bias: bfloat16 [2304], P(('wide', 'narrow')), may hold values from -2 to 2
- short_kernel: bfloat16 [3, 2304], P(None, ('wide', 'narrow')), may hold values from -3 to 3
- cond_kernel: bfloat16 [3, 768], P(None, ('wide', 'narrow')), may hold values from -3 to 3
- fourier_gain: bfloat16 [2, 768], P(None, ('wide', 'narrow')), may hold values from -4 to 4
- out_weight: bfloat16 [768, 768], P('wide', 'narrow'), may hold values from -0.21875 to 0.21875
- out_bias: bfloat16 [768], P(('wide', 'narrow')), may hold values from -2 to 2
- gain_first: bfloat16 [768], P(('wide', 'narrow')), may hold values from 0.099609375 to 1.8984375
- bias_first: bfloat16 [768], P(('wide', 'narrow')), may hold values from -2 to 2
- gain_second: bfloat16 [768], P(('wide', 'narrow')), may hold values from 0.099609375 to 1.8984375
- bias_second: bfloat16 [768], P(('wide', 'narrow')), may hold values from -2 to 2
- gate_weight: bfloat16 [768, 3072], P('wide', 'narrow'), may hold values from -0.21875 to 0.21875
- up_weight: bfloat16 [768, 3072], P('wide', 'narrow'), may hold values from -0.21875 to 0.21875
- glu_bias: bfloat16 [2, 3072], P(None, ('wide', 'narrow')), may hold values from -2 to 2
- down_weight: bfloat16 [3072, 768], P('wide', 'narrow'), may hold values from -0.109375 to 0.109375
- down_bias: bfloat16 [768], P(('wide', 'narrow')), may hold values from -2 to 2
- cotan_short: bfloat16 [32, 128, 768], P(('wide', 'narrow')), may hold values from -6 to 6
- cotan_long: bfloat16 [32, 512, 768], P(('wide', 'narrow')), may hold values from -6 to 6
Outputs:
- output_short: bfloat16 [32, 128, 768], P(('wide', 'narrow'))
- output_long: bfloat16 [32, 512, 768], P(('wide', 'narrow'))
- input_grad_short: float32 [32, 128, 768], P(('wide', 'narrow'))
- input_grad_long: float32 [32, 512, 768], P(('wide', 'narrow'))
- grad_in_weight: float32 [768, 2304], P('wide', 'narrow')
- grad_in_bias: float32 [2304], P(('wide', 'narrow'))
- grad_short_kernel: float32 [3, 2304], P(None, ('wide', 'narrow'))
- grad_cond_kernel: float32 [3, 768], P(None, ('wide', 'narrow'))
- grad_fourier_gain: float32 [2, 768], P(None, ('wide', 'narrow'))
- grad_out_weight: float32 [768, 768], P('wide', 'narrow')
- grad_out_bias: float32 [768], P(('wide', 'narrow'))
- grad_gain_first: float32 [768], P(('wide', 'narrow'))
- grad_bias_first: float32 [768], P(('wide', 'narrow'))
- grad_gain_second: float32 [768], P(('wide', 'narrow'))
- grad_bias_second: float32 [768], P(('wide', 'narrow'))
- grad_gate_weight: float32 [768, 3072], P('wide', 'narrow')
- grad_up_weight: float32 [768, 3072], P('wide', 'narrow')
- grad_glu_bias: float32 [2, 3072], P(None, ('wide', 'narrow'))
- grad_down_weight: float32 [3072, 768], P('wide', 'narrow')
- grad_down_bias: float32 [768], P(('wide', 'narrow'))
All inputs are finite; a program needn't handle non-finite values.
Results may differ from a plain program's by a relative error of at most 0.017.
Values may be sent and summed in bfloat16 or wider, within the bound.
A program may use at most 192 MiB of HBM per device.

v0:
```python
import functools
import math

import jax
import jax.numpy as jnp
import numpy as np
from jax import lax
from jax.experimental import pallas as pl
from jax.experimental.pallas import tpu as pltpu
from jax.sharding import PartitionSpec as P

bf16 = jnp.bfloat16
f32 = jnp.float32
MESH = pl.DeviceIdType.MESH
Z = 4
D = 768
BLK = 256
PAD = 8


def coords():
    w = lax.axis_index("wide")
    return w // 4, (w // 2) % 2, w % 2, lax.axis_index("narrow")


def flat(z, x, c):
    return (z * 2 + x) * 2 + c


def window(ref, rows, cols, w, y):
    return ref.at[
        pl.ds(pl.multiple_of(w * rows, 16), rows), pl.ds(pl.multiple_of(y * cols, 128), cols)
    ]


def greet(peers):
    barrier = pltpu.get_barrier_semaphore()
    for peer in peers:
        pl.semaphore_signal(barrier, inc=1, device_id=peer, device_id_type=MESH)
    pl.semaphore_wait(barrier, len(peers))


def neighbours():
    z, x, c, y = coords()
    zpeers = [(flat(lax.rem(z + i, Z), x, c), y) for i in (1, 2, 3)]
    return zpeers, (flat(z, 1 - x, c), y), (flat(z, x, c), 1 - y), (flat(z, x, 1 - c), y)


class Gather:
    def __init__(self, items, ici_send, ici_recv, core_send, core_recv, own_sem):
        self.items = items
        self.ici_send, self.ici_recv = ici_send, ici_recv
        self.core_send, self.core_recv, self.own_sem = core_send, core_recv, own_sem
        self.z, self.x, self.c, self.y = coords()
        self.zpeers, self.xpeer, self.ypeer, self.cpeer = neighbours()
        self.count = [0] * len(items)
        self.pending = []

    def shard(self, k):
        ref, _, first, cols = self.items[k]
        return ref if cols == ref.shape[1] else ref.at[:, first : first + cols]

    def view(self, k, i, xf, yf, cf=0):
        ref, full, first, cols = self.items[k]
        zz = lax.rem(self.z + i, Z)
        xx = 1 - self.x if xf else self.x
        yy = 1 - self.y if yf else self.y
        cc = 1 - self.c if cf else self.c
        rows, whole = ref.shape
        row = pl.multiple_of(flat(zz, xx, cc) * rows, 16)
        return full.at[pl.ds(row, rows), pl.ds(pl.multiple_of(yy * whole + first, 128), cols)]

    def copy(self, k, src, dst, peer, send, recv):
        return pltpu.make_async_remote_copy(
            src_ref=src, dst_ref=dst, send_sem=send, recv_sem=recv, device_id=peer, device_id_type=MESH
        )

    def post(self, k, i, xf, yf, peer, send, recv):
        src = self.shard(k) if (i, xf, yf) == (0, 0, 0) else self.view(k, i, xf, yf)
        self.pending.append((k, send))
        self.copy(k, src, self.view(k, i, xf, yf), peer, self.sent(k, send), recv).start()

    def sent(self, k, send):
        return (self.core_send if send[0] else self.ici_send).at[k, send[1]]

    def send(self, k, i, xf, yf, peer, slot):
        self.post(k, i, xf, yf, peer, (0, self.count[k]), self.ici_recv.at[k, slot])
        self.count[k] += 1

    def to_core(self, k, i, xf, yf):
        slot = i * 4 + xf * 2 + yf
        self.post(k, i, xf, yf, self.cpeer, (1, slot), self.core_recv.at[k, slot])

    def arrived(self, k, i, xf, yf, cf=0):
        slot = i * 4 + xf * 2 + yf
        sems = self.core_recv if cf else self.ici_recv
        dst = self.view(k, i, xf, yf, cf)
        self.copy(k, self.shard(k), dst, self.cpeer, self.ici_send.at[k, 0], sems.at[k, slot]).wait_recv()

    def own(self, k):
        return pltpu.make_async_copy(self.shard(k), self.view(k, 0, 0, 0), self.own_sem.at[k])

    def start(self, k):
        self.own(k).start()
        for i in (1, 3, 2):
            self.send(k, 0, 0, 0, self.zpeers[i - 1], ((Z - i) % Z) * 4)
        self.send(k, 0, 0, 0, self.xpeer, 2)
        self.send(k, 0, 0, 0, self.ypeer, 1)
        self.to_core(k, 0, 0, 0)

    def events(self, order):
        out = []
        for kind, k in order:
            if kind == "S":
                out.append(functools.partial(self.start, k))
            elif kind == "z":
                out += [functools.partial(self.zstep, k, i) for i in (1, 3, 2)]
            elif kind == "p":
                out += [functools.partial(self.xystep, k, i, xf) for i in (0, 1, 3, 2) for xf in (1, 0)]
            else:
                out += [functools.partial(self.dstep, k, i) for i in (0, 1, 3, 2)]
        return out

    def zstep(self, k, i):
        self.arrived(k, i, 0, 0)
        self.send(k, i, 0, 0, self.xpeer, i * 4 + 2)
        self.send(k, i, 0, 0, self.ypeer, i * 4 + 1)
        self.to_core(k, i, 0, 0)

    def xystep(self, k, i, xf):
        self.arrived(k, i, xf, 1 - xf)
        if i % 2 == 1 - xf:
            self.send(k, i, xf, 1 - xf, self.ypeer if xf else self.xpeer, i * 4 + 3)
        self.to_core(k, i, xf, 1 - xf)

    def dstep(self, k, i):
        self.arrived(k, i, 1, 1)
        self.to_core(k, i, 1, 1)

    def done(self, k):
        self.own(k).wait()
        for i in range(4):
            for xf in range(2):
                for yf in range(2):
                    self.arrived(k, i, xf, yf, 1)

    def finish(self):
        for k, send in self.pending:
            dst = self.view(k, 0, 0, 0)
            self.copy(k, self.shard(k), dst, self.cpeer, self.sent(k, send), self.ici_recv.at[k, 0]).wait_send()


def normal(v):
    centred = v - jnp.mean(v, axis=-1, keepdims=True)
    scale = lax.rsqrt(jnp.mean(centred * centred, axis=-1, keepdims=True) + 1e-5)
    return centred * scale, scale


def dot(a, b):
    return jnp.dot(a, b, preferred_element_type=f32)


def dot_nt(a, b):
    return lax.dot_general(a, b, (((1,), (1,)), ((), ())), preferred_element_type=f32)


def fold(v):
    return jnp.sum(v.reshape(v.shape[0] // 8, 8, v.shape[1]), axis=0)


def loop(count, fn):
    def go(i, carry):
        fn(i)
        return carry

    lax.fori_loop(0, count, go, 0)


def rows_at(i, size):
    return pl.ds(pl.multiple_of(i * size, size), size)


GELU_A = math.sqrt(2.0 / math.pi)
GELU_B = 0.044715


class Rows:
    def __init__(self, short, long):
        self.short, self.long = short, long
        self.total = short + long
        self.padded = self.total + 3 * PAD
        self.segs = ((0, short, PAD), (short, long, 2 * PAD + short))
        self.chunk = short
        self.count = self.total // short
        self.half = short // 2

    def plain(self, i):
        return rows_at(i, self.chunk)

    def place(self, i):
        return pl.multiple_of(i * self.chunk + PAD + PAD * jnp.minimum(i, 1), PAD)

    def halves(self, i):
        low = jnp.where(i == 0, 0, self.short + (i - 1) * self.half)
        high = low + jnp.where(i == 0, self.half, self.long // 2)
        return tuple(pl.ds(pl.multiple_of(v, self.half), self.half) for v in (low, high))


def window3(ref, p, n):
    span = ref[pl.ds(pl.multiple_of(p - PAD, PAD), n + 2 * PAD), :]
    return span[PAD - 1 : PAD - 1 + n], span[PAD : PAD + n], span[PAD + 1 : PAD + 1 + n]


def taps3(views, taps, flip=False):
    a, b, c = views
    return taps[0] * (c if flip else a) + taps[1] * b + taps[2] * (a if flip else c)


def owners(width, q):
    row = lax.broadcasted_iota(jnp.int32, (32, D), 0)
    owner = 2 * (row % 16) + row // 16
    col = lax.broadcasted_iota(jnp.int32, (32, D), 1) + q * D - owner * width
    return jnp.logical_and(col >= 0, col < width)


def one_hot(width, q):
    col = lax.broadcasted_iota(jnp.int32, (8, D), 1) + q * D
    whole = jnp.floor((col.astype(f32) + 0.5) * (1.0 / width)).astype(jnp.int32)
    place = (col - whole * width)[0:1]
    hit = lax.broadcasted_iota(jnp.int32, (128, D), 0) == place
    return jnp.where(hit, 1.0, 0.0).astype(bf16)


def unpack(wide_ref, first, count, width, out_ref):
    parts = []
    for r in range(first, first + count):
        for y in range(2):
            parts.append(wide_ref.at[y][pl.ds(r, 16, stride=32), :])
    parts = jnp.concatenate(parts, axis=0).astype(bf16)
    for q in range(32 * width // D):
        spread = dot(parts, one_hot(width, q))
        mine = owners(width, q)
        for r in range(count):
            piece = jnp.where(mine, spread[32 * r : 32 * r + 32], 0.0)
            out_ref[r : r + 1, q * D : (q + 1) * D] = jnp.sum(piece, axis=0, keepdims=True)


def repack(vec, count, width, first, out_ref):
    out = None
    for q in range(32 * width // D):
        mine = owners(width, q)
        highs, lows = [], []
        for r in range(count):
            v = jnp.where(mine, vec[r : r + 1, q * D : (q + 1) * D], 0.0)
            high = v.astype(bf16)
            highs.append(high)
            lows.append((v - high.astype(f32)).astype(bf16))
        value = dot_nt(jnp.concatenate(highs + lows, axis=0), one_hot(width, q))
        out = value if out is None else out + value
    n = 32 * count
    for r in range(count):
        v = out[32 * r : 32 * r + 32] + out[n + 32 * r : n + 32 * r + 32]
        for y in range(2):
            out_ref.at[y][pl.ds(first + r, 16, stride=24), :] = v[16 * y : 16 * y + 16]


STEP = 16


def angle_parts(length):
    t = np.arange(length)
    coarse = 2.0 * np.pi * (np.outer(STEP * np.arange(length // 2 // STEP), t) % length) / length
    fine = 2.0 * np.pi * (np.outer(np.arange(STEP), t) % length) / length
    scale = 1.0 / math.sqrt(length)
    parts = [np.cos(coarse) * scale, np.sin(coarse) * scale, np.cos(fine), np.sin(fine)]
    return np.concatenate(parts).astype(np.float32)


def build_table(parts_ref, out_ref):
    length = out_ref.shape[0]
    n = length // 2 // STEP
    fine_cos, fine_sin = parts_ref[2 * n : 2 * n + STEP], parts_ref[2 * n + STEP : 2 * n + 2 * STEP]
    row = lax.broadcasted_iota(jnp.int32, (STEP, length), 0)
    sign = 1.0 - 2.0 * (lax.broadcasted_iota(jnp.int32, (STEP, length), 1) % 2).astype(f32)
    for i in range(n):
        cos, sin = parts_ref[i : i + 1], parts_ref[n + i : n + i + 1]
        low = -(sin * fine_cos + cos * fine_sin)
        if i == 0:
            low = jnp.where(row == 0, sign / math.sqrt(length), low)
        out_ref[i * STEP : (i + 1) * STEP] = (cos * fine_cos - sin * fine_sin).astype(bf16)
        out_ref[length // 2 + i * STEP : length // 2 + (i + 1) * STEP] = low.astype(bf16)


def forward_kernel(shape, widths, *refs):
    (pack, w0, w1, w2, w3, w4, ts, tl, cs, cl, ps, pl_) = refs[:12]
    (g_in, g_out, g_gate, g_up, g_down, v72, v24, v96, o_n1, o_proj, o_spec, o_carr, o_long,
     o_mixed, o_hid, o_n2, o_pd, o_ga, o_ap, o_ge, o_fs, o_fst, o_fl, o_flt) = refs[12:36]
    (f_small, f_in, f_out, f_gate, f_up, smallw, x, cot, n1, n1t, proj, spec, carr, longc,
     mixed, mixedt, hid, n2, n2t, ga, ap, ge, pd, pj, gl, vap, rhs, tr, prod, s_ps, s_pl, s_fs, s_fst,
     s_fl, s_flt, ici_send, ici_recv, core_send, core_recv, own_sem, load_sem, save_sem) = refs[36:]
    rows = shape.total
    short = shape.short
    zp, xp, yp, cp = neighbours()
    greet(zp + [xp, yp, cp])
    items = [(pack, f_small), (w0, f_in), (w1, f_out), (w2, f_gate), (w3, f_up), (w4, g_down)]
    g = Gather([(a, b, 0, a.shape[1]) for a, b in items], ici_send, ici_recv, core_send, core_recv, own_sem)
    steps = g.events(GATHER_ORDER)
    marks = {}
    for token in GATHER_ORDER:
        size = {"S": 1, "z": 3, "p": 8, "d": 4}[token[0]]
        marks[token] = size + (max(marks.values()) if marks else 0)
    position = [0]

    def pump(n):
        for step in steps[position[0] : position[0] + n]:
            step()
        position[0] = min(position[0] + n, len(steps))

    def need(k):
        pump(max(0, marks["d", k] - position[0]))
        g.done(k)

    pump(GATHER_FIRST)
    loads = []
    for a, b in [(ps, s_ps), (pl_, s_pl), (ts, x.at[0:short]), (tl, x.at[short:rows]),
                 (cs, cot.at[0:short]), (cl, cot.at[short:rows])]:
        copy = pltpu.make_async_copy(a, b, load_sem.at[len(loads)])
        copy.start()
        loads.append(copy)
    saves = []

    def save(a, b):
        copy = pltpu.make_async_copy(a, b, save_sem.at[len(saves)])
        copy.start()
        saves.append(copy)

    for start, length, place in shape.segs:
        zero = jnp.zeros((PAD, BLK), f32)
        for ref in (pj.at[0], pj.at[1], pj.at[2], vap):
            ref[place - PAD : place] = zero
            ref[place + length : place + length + PAD] = zero
    for copy in loads:
        copy.wait()
    build_table(s_ps, s_fs)
    build_table(s_pl, s_fl)
    pump(6)
    s_fst[...] = s_fs[...].T
    s_flt[...] = s_fl[...].T
    for a, b in ((s_fs, o_fs), (s_fst, o_fst), (s_fl, o_fl), (s_flt, o_flt)):
        save(a, b)
    need(0)
    for y in range(2):
        smallw[y] = f_small[:, y * 128 : (y + 1) * 128].astype(f32)
    unpack(smallw, 0, 4, widths[0], v72)
    pump(2)
    unpack(smallw, 4, 11, widths[1], v24)
    unpack(smallw, 15, 2, widths[2], v96)
    pump(2)

    def norm_one(i):
        r = rows_at(i, 64)
        h, _ = normal(x[r, :].astype(f32))
        n1[r, :] = (h * v24[6:7, :] + v24[7:8, :]).astype(bf16)

    loop(rows // 64, norm_one)
    pump(2)
    n1t[...] = n1[...].T
    save(n1t, o_n1)
    need(1)
    save(f_in, g_in)

    def mix(j, pumps):
        ch = slice(j * BLK, (j + 1) * BLK)
        los = [b * D + j * BLK for b in range(3)]
        tap = [[v72[1 + k : 2 + k, lo : lo + BLK] for k in range(3)] for lo in los]
        ctap = [v24[k : k + 1, ch] for k in range(3)]
        inner, outer = v24[3:4, ch], v24[4:5, ch]
        for b, lo in enumerate(los):
            value = dot(n1[...], f_in[:, lo : lo + BLK]) + v72[0:1, lo : lo + BLK]
            proj[:, lo : lo + BLK] = value.astype(bf16)
            for start, length, place in shape.segs:
                pj[b, place : place + length] = value[start : start + length]
        pump(pumps[0])
        n = shape.chunk

        def convolve(i):
            r, p = shape.plain(i), shape.place(i)
            here = pl.ds(p, n)
            gl[r, :] = taps3(window3(pj.at[0], p, n), tap[0])
            value = taps3(window3(pj.at[2], p, n), tap[2])
            vap[here, :] = value
            rhs[r, BLK:] = (taps3(window3(pj.at[1], p, n), tap[1]) * value).astype(bf16)

        def condition(i):
            rhs[shape.plain(i), :BLK] = taps3(window3(vap, shape.place(i), n), ctap).astype(bf16)

        loop(shape.count, convolve)
        loop(shape.count, condition)
        pump(pumps[1])
        for (start, length, _), table in zip(shape.segs, (s_fs, s_fl)):
            tr[start : start + length] = dot(table[...], rhs[start : start + length])

        def filt(i):
            a, b = shape.halves(i)
            sa, sb = tr[a, :BLK], tr[b, :BLK]
            ca, cb = tr[a, BLK:], tr[b, BLK:]
            spec[a, ch] = sa.astype(bf16)
            spec[b, ch] = sb.astype(bf16)
            carr[a, ch] = ca.astype(bf16)
            carr[b, ch] = cb.astype(bf16)
            fa = jnp.tanh(sa * inner) * outer
            fb = jnp.tanh(sb * inner) * outer
            real, imag = fa * ca, fb * cb
            row = lax.broadcasted_iota(jnp.int32, real.shape, 0)
            first = jnp.logical_and(row == 0, i <= 1)
            prod[a, :] = jnp.where(first, real, 2.0 * (real - imag)).astype(bf16)
            prod[b, :] = jnp.where(first, imag, 2.0 * (fa * cb + fb * ca)).astype(bf16)

        loop(shape.count, filt)
        pump(pumps[2])
        for (start, length, _), table in zip(shape.segs, (s_fst, s_flt)):
            value = dot(table[...], prod[start : start + length])
            longc[start : start + length, ch] = value.astype(bf16)
            mixed[start : start + length, ch] = (value * gl[start : start + length]).astype(bf16)

    for j in range(3):
        mix(j, MIX_PUMPS[j])
    for a, b in ((proj, o_proj), (spec, o_spec), (carr, o_carr), (longc, o_long)):
        save(a, b)
    pump(3)
    mixedt[...] = mixed[...].T
    save(mixedt, o_mixed)
    need(2)
    save(f_out, g_out)

    def branch_one(i):
        r = rows_at(i, 128)
        value = x[r, :].astype(f32) + dot(mixed[r, :], f_out[...]) + v24[5:6, :]
        hid[r, :] = value
        h, _ = normal(value)
        n2[r, :] = (h * v24[8:9, :] + v24[9:10, :]).astype(bf16)

    loop(rows // 128, branch_one)
    save(hid, o_hid)
    n2t[...] = n2[...].T
    save(n2t, o_n2)

    def glu(i):
        cols = rows_at(i, BLK)
        for m in range(0, rows, 320):
            gate = dot(n2[m : m + 320, :], f_gate[:, cols]) + v96[0:1, cols]
            up = dot(n2[m : m + 320, :], f_up[:, cols]) + v96[1:2, cols]
            square = gate * gate
            t = jnp.tanh(gate * (GELU_A + GELU_A * GELU_B * square))
            half = 0.5 * (1.0 + t)
            act = gate * half
            slope = half + 0.5 * gate * (1.0 - t * t) * (GELU_A + 3.0 * GELU_A * GELU_B * square)
            ga[m : m + 320, cols] = (act * up).astype(bf16)
            ge[m : m + 320, cols] = act.astype(bf16)
            ap[m : m + 320, cols] = (up * slope).astype(bf16)
        pd[cols, :] = dot(ga[:, cols].T, cot[...]).astype(bf16)

    need(3)
    save(f_gate, g_gate)
    need(4)
    save(f_up, g_up)
    tiles = ga.shape[1] // BLK

    def tile(i):
        glu(i)
        for q, n in enumerate(GLU_PUMPS):
            if n:
                pl.when(i == q)(functools.partial(pump, n))
        pl.when(i == tiles // 2 - 1)(save_first)

    def save_first():
        half = pd.shape[0] // 2
        first = slice(0, half)
        pairs = [(a.at[:, first], b.at[:, first]) for a, b in ((ga, o_ga), (ap, o_ap), (ge, o_ge))]
        for k, (a, b) in enumerate(pairs + [(pd.at[first], o_pd.at[first])]):
            pltpu.make_async_copy(a, b, load_sem.at[k]).start()

    loop(tiles, tile)
    half = pd.shape[0] // 2
    rest = slice(half, 2 * half)
    for a, b in ((ga, o_ga), (ap, o_ap), (ge, o_ge)):
        save(a.at[:, rest], b.at[:, rest])
    save(pd.at[rest], o_pd.at[rest])
    first = slice(0, half)
    early = [(a.at[:, first], b.at[:, first]) for a, b in ((ga, o_ga), (ap, o_ap), (ge, o_ge))]
    early.append((pd.at[first], o_pd.at[first]))
    for k, (a, b) in enumerate(early):
        pltpu.make_async_copy(a, b, load_sem.at[k]).wait()
    need(5)
    for copy in saves:
        copy.wait()
    g.finish()


GATHER_ORDER = (
    ("S", 0), ("S", 1), ("S", 2), ("z", 0), ("z", 1), ("p", 0), ("S", 3), ("d", 0), ("z", 2), ("p", 1), ("d", 1),
    ("z", 3), ("p", 2), ("S", 4), ("d", 2), ("p", 3), ("z", 4), ("S", 5), ("d", 3), ("p", 4), ("z", 5), ("d", 4),
    ("p", 5), ("d", 5),
)
GATHER_FIRST = 3
MIX_PUMPS = ((3, 3, 3), (4, 4, 4), (5, 5, 5))
GLU_PUMPS = (0, 2, 0, 2, 0, 2, 0, 2, 0, 2, 0, 2)


def place_rows(piece, first):
    rows, width = piece.shape
    return lax.pad(piece, jnp.zeros((), piece.dtype), ((first, 32 - first - rows, 0), (0, 128 - width, 0)))


LARGE = (0, 5, 11, 12, 14)
SMALL = (1, 2, 3, 4, 6, 7, 8, 9, 10, 15, 13)


def pack_small(shards):
    total = None
    first = 0
    for i in SMALL:
        piece = shards[i].reshape(-1, shards[i].shape[-1])
        placed = place_rows(piece, first)
        first += piece.shape[0]
        total = placed if total is None else total + placed
    return total


def forward(ts, tl, cs, cl, shards):
    shape = Rows(ts.shape[1], tl.shape[1])
    short, long, rows = shape.short, shape.long, shape.total
    widths = (shards[1].shape[0], shards[6].shape[0], shards[13].shape[1])
    large = [shards[i] for i in LARGE]
    ff = shards[11].shape[1] * 2
    full = [(16 * s.shape[0], 2 * s.shape[1]) for s in large]
    S = jax.ShapeDtypeStruct
    V = pltpu.VMEM
    angles = [angle_parts(short), angle_parts(long)]
    ins = [pack_small(shards)] + large + [ts.reshape(short, D), tl.reshape(long, D)]
    ins += [cs.reshape(short, D), cl.reshape(long, D)] + [jnp.asarray(a) for a in angles]
    square = [(n, n) for n in (short, short, long, long)]
    vecs = [(8, 32 * widths[0]), (16, 32 * widths[1]), (8, 32 * widths[2])]
    outs = [S(s, bf16) for s in full] + [S(s, f32) for s in vecs]
    outs += [S((D, rows), bf16), S((rows, 3 * D), bf16)] + [S((rows, D), bf16)] * 3
    outs += [S((D, rows), bf16), S((rows, D), f32), S((D, rows), bf16), S((ff, D), bf16)]
    outs += [S((rows, ff), bf16)] * 3 + [S(s, bf16) for s in square]
    any_ = pl.BlockSpec(memory_space=pl.ANY)
    vm = pl.BlockSpec(memory_space=pltpu.VMEM)
    sem = pltpu.SemaphoreType.DMA
    scratch = [V((512, 256), bf16)] + [V(s, bf16) for s in full[:4]]
    scratch += [V((2, 512, 128), f32), V((rows, D), bf16), V((rows, D), bf16), V((rows, D), bf16), V((D, rows), bf16)]
    scratch += [V((rows, 3 * D), bf16)] + [V((rows, D), bf16)] * 4
    scratch += [V((D, rows), bf16), V((rows, D), f32), V((rows, D), bf16), V((D, rows), bf16)]
    scratch += [V((rows, ff), bf16)] * 3 + [V((ff, D), bf16)]
    scratch += [V((3, shape.padded, BLK), f32), V((rows, BLK), f32), V((shape.padded, BLK), f32)]
    scratch += [V((rows, 2 * BLK), bf16), V((rows, 2 * BLK), f32), V((rows, BLK), bf16)]
    scratch += [V(a.shape, f32) for a in angles] + [V(s, bf16) for s in square]
    scratch += [sem((6, 15)), sem((6, 16)), sem((6, 16)), sem((6, 16)), sem((6,)), sem((6,)), sem((28,))]
    return pl.pallas_call(
        functools.partial(forward_kernel, shape, widths),
        out_shape=outs,
        in_specs=[any_] * len(ins),
        out_specs=[any_] * 5 + [vm] * 3 + [any_] * 16,
        scratch_shapes=scratch,
        compiler_params=pltpu.CompilerParams(collective_id=0, has_side_effects=True, vmem_limit_bytes=67043328),
    )(*ins)


class Reduce:
    def __init__(self, items, send_sem, recv_sem, own_sem):
        self.items = items
        self.send_sem, self.recv_sem, self.own_sem = send_sem, recv_sem, own_sem
        self.z, self.x, self.c, self.y = coords()
        self.zpeers, self.xpeer, self.ypeer, self.cpeer = neighbours()
        self.count = [0] * len(items)
        self.pending = []

    def post(self, k, src, dst, peer, slot):
        copy = pltpu.make_async_remote_copy(
            src_ref=src,
            dst_ref=dst,
            send_sem=self.send_sem.at[k, self.count[k]],
            recv_sem=self.recv_sem.at[k, slot],
            device_id=peer,
            device_id_type=MESH,
        )
        self.pending.append((k, self.count[k]))
        self.count[k] += 1
        copy.start()

    def arrived(self, k, dst, slot):
        pltpu.make_async_remote_copy(
            src_ref=dst,
            dst_ref=dst,
            send_sem=self.send_sem.at[k, 0],
            recv_sem=self.recv_sem.at[k, slot],
            device_id=self.cpeer,
            device_id_type=MESH,
        ).wait_recv()

    def part(self, k, b, core, yy):
        item = self.items[k]
        start = (2 * b + core) * item["rows"] + item["base"]
        rows = pl.ds(pl.multiple_of(start, 8), item["rows"])
        if item["flat"]:
            cols = item["cols"]
            return item["source"].at[rows, pl.ds(pl.multiple_of(yy * cols, 128), cols)]
        return item["source"].at[yy, rows, pl.ds(item["first"], item["cols"])]

    def own(self, k, b, yy):
        held = self.items[k]["held"]
        return held.at[b, yy] if held is not None else self.part(k, b, self.c, yy)

    def block(self, i, xx):
        return lax.rem(self.z + i, Z) * 2 + xx

    def order(self):
        for i in (1, 3, 2, 0):
            yield i, self.block(i, 1 - self.x), self.block(i, self.x)

    def core(self, k):
        item = self.items[k]
        for i, across, along in self.order():
            for b in (across, along):
                for yy in range(2):
                    self.post(k, self.part(k, b, 1 - self.c, yy), item["core"].at[b, yy], self.cpeer, b)
        if item["held"] is not None:
            for i, across, along in self.order():
                for b in (across, along):
                    for yy in range(2):
                        pltpu.make_async_copy(
                            self.part(k, b, self.c, yy), item["held"].at[b, yy], self.own_sem.at[b, yy]
                        ).start()

    def merge(self, k, b):
        item = self.items[k]
        if item["held"] is not None:
            for yy in range(2):
                pltpu.make_async_copy(
                    self.part(k, b, self.c, yy), item["held"].at[b, yy], self.own_sem.at[b, yy]
                ).wait()
        self.arrived(k, item["core"].at[b], b)
        for yy in range(2):
            own = self.own(k, b, yy)
            own[...] = own[...] + item["core"][b, yy]

    def diag(self, k):
        item = self.items[k]
        for i, across, along in self.order():
            self.merge(k, across)
            src = self.own(k, across, 1 - self.y)
            if i % 2 == 0:
                self.post(k, src, item["diag_x"].at[i // 2], self.xpeer, 8 + i // 2)
            else:
                self.post(k, src, item["diag_y"].at[i // 2], self.ypeer, 10 + i // 2)
        for i, across, along in self.order():
            self.merge(k, along)

    def near(self, k):
        item = self.items[k]
        for i, across, along in self.order():
            own = self.own(k, along, 1 - self.y)
            if i % 2 == 0:
                self.arrived(k, item["diag_x"].at[i // 2], 8 + i // 2)
                own[...] = own[...] + item["diag_x"][i // 2]
            self.post(k, own, item["near_y"].at[i], self.ypeer, 12 + i)
            own = self.own(k, across, self.y)
            if i % 2 == 1:
                self.arrived(k, item["diag_y"].at[i // 2], 10 + i // 2)
                own[...] = own[...] + item["diag_y"][i // 2]
            self.post(k, own, item["near_x"].at[i], self.xpeer, 16 + i)

    def far(self, k):
        item = self.items[k]
        for i, across, along in self.order():
            self.arrived(k, item["near_x"].at[i], 16 + i)
            self.arrived(k, item["near_y"].at[i], 12 + i)
            own = self.own(k, along, self.y)
            total = own[...].astype(f32) + item["near_x"][i].astype(f32) + item["near_y"][i].astype(f32)
            own[...] = total.astype(own.dtype)
            if i:
                self.post(k, own, item["far"].at[i - 1], self.zpeers[i - 1], 19 + i)

    def last(self, k):
        item = self.items[k]
        total = self.own(k, self.block(0, self.x), self.y)[...].astype(f32)
        for i in range(3):
            self.arrived(k, item["far"].at[i], 20 + i)
            total = total + item["far"][i].astype(f32)
        item["out"][...] = total

    def finish(self):
        for k, count in self.pending:
            rest = self.items[k]["far"].at[0]
            pltpu.make_async_remote_copy(
                src_ref=rest,
                dst_ref=rest,
                send_sem=self.send_sem.at[k, count],
                recv_sem=self.recv_sem.at[k, 0],
                device_id=self.cpeer,
                device_id_type=MESH,
            ).wait_send()


def backward_kernel(shape, widths, *refs):
    (pd, h_g, h_u, h_d, h_o, h_i, ts, tl, cs, cl, v72, v24, r_n1, r_proj, r_spec, r_carr, r_long,
     r_mixed, r_hid, r_n2, r_ga, r_ap, r_ge, fs, fst, fl, flt) = refs[:27]
    y_s, y_l, o_s, o_l, o_in, o_out, o_gate, o_up, o_down, o_small = refs[27:37]
    nitem = 10
    groups = [refs[37 + q * nitem : 37 + (q + 1) * nitem] for q in range(6)]
    (held, wd, wg, wu, wo, wi, p_small, cot, n2t, apb, geb, acc, big, gm, mixedt, gpj, bspec, bcarr, blong,
     pj, dco, vap, gr, dcp, rhs, tr, s_fs, s_fst, s_fl, s_flt, g72, g24, g96,
     send_sem, recv_sem, own_sem, load_sem, tile_sem, blk_sem, out_sem) = refs[37 + 6 * nitem :]
    rows, short = shape.total, shape.short
    zp, xp, yp, cp = neighbours()
    greet(zp + [xp, yp, cp])

    def item(k, source, out, nrows, cols, first=0, base=0, flat_form=False, held=None):
        names = ("core", "diag_x", "diag_y", "near_x", "near_y", "far")
        made = dict(source=source, out=out, rows=nrows, cols=cols, first=first, base=base, flat=flat_form, held=held)
        made.update({name: group[k] for name, group in zip(names, groups)})
        return made

    half = wg.shape[2] // 2
    span = wi.shape[2] // 3
    n = wi.shape[1]
    r_gate, r_in = o_gate.shape[0], o_in.shape[0]
    items = [
        item(0, pd, o_down, o_down.shape[0], o_down.shape[1], flat_form=True, held=held),
        item(1, wg, o_gate.at[:, 0:half], r_gate, half),
        item(2, wu, o_up.at[:, 0:half], r_gate, half),
        item(3, wg, o_gate.at[:, half : 2 * half], r_gate, half, first=half),
        item(4, wu, o_up.at[:, half : 2 * half], r_gate, half, first=half),
        item(5, wo, o_out, o_out.shape[0], o_out.shape[1]),
    ]
    for t in range(3):
        out = o_in.at[:, t * span : (t + 1) * span]
        items.append(item(6 + t, wd, out, r_in, span, base=t * n, flat_form=True))
    items.append(item(9, p_small, o_small, o_small.shape[0], o_small.shape[1]))
    red = Reduce(items, send_sem, recv_sem, own_sem)
    red.core(0)
    loads = {}

    def load(name, a, b):
        copy = pltpu.make_async_copy(a, b, load_sem.at[len(loads)])
        copy.start()
        loads[name] = copy

    def wait(*names):
        for name in names:
            loads[name].wait()

    def halves(name, a, b, first, size):
        cols = b.shape[2]
        for y in range(2):
            lo = y * cols + first
            load(name + str(y), a.at[:, lo : lo + size], b.at[y, :, first : first + size])

    load("cs", cs, cot.at[0:short])
    load("cl", cl, cot.at[short:rows])
    load("n2t", r_n2, n2t)
    quarter = wd.shape[0] // 4
    for q in (0, 2):
        load("wd%d" % q, h_d.at[q * quarter : (q + 1) * quarter], wd.at[q * quarter : (q + 1) * quarter])
    halves("ga", h_g, wg, 0, half)
    halves("ua", h_u, wu, 0, half)
    per = 2 * (half // BLK)
    total_tiles = 2 * per

    def tile_start(i):
        h, t, y = i // per, lax.rem(i, per) // 2, lax.rem(i, 2)
        return h * half + t * BLK, y

    def tile_copy(i, which):
        first, y = tile_start(i)
        cols = pl.ds(pl.multiple_of(y * 2 * half + first, BLK), BLK)
        slot = lax.rem(i, 2)
        src, dst = ((r_ap, apb), (r_ge, geb))[which]
        return pltpu.make_async_copy(src.at[:, cols], dst.at[slot], tile_sem.at[which, slot])

    for which in range(2):
        tile_copy(0, which).start()
    for q in (1, 3):
        load("wd%d" % q, h_d.at[q * quarter : (q + 1) * quarter], wd.at[q * quarter : (q + 1) * quarter])
    halves("gb", h_g, wg, half, half)
    halves("ub", h_u, wu, half, half)
    load("hid", r_hid, big)
    wide3 = gpj.shape[1]
    load("ga_a", r_ga.at[:, 0:wide3], gpj)
    load("ga_b", r_ga.at[:, wide3:], gm)
    load("mixedt", r_mixed, mixedt)
    halves("wo", h_o, wo, 0, wo.shape[2])
    halves("wi", h_i, wi, 0, wi.shape[2])
    for name, a, b in (("fs", fs, s_fs), ("fst", fst, s_fst), ("fl", fl, s_fl), ("flt", flt, s_flt)):
        load(name, a, b)

    def block_copies(j):
        ch = slice(j * BLK, (j + 1) * BLK)
        return [
            pltpu.make_async_copy(src.at[:, ch], dst, blk_sem.at[k])
            for k, (src, dst) in enumerate(((r_spec, bspec), (r_carr, bcarr), (r_long, blong)))
        ]

    for copy in block_copies(0):
        copy.start()
    acc[...] = jnp.zeros_like(acc)
    zero = jnp.zeros((PAD, BLK), f32)
    for start, length, place in shape.segs:
        for ref in (pj.at[0], pj.at[1], pj.at[2], dco, vap, dcp):
            ref[place - PAD : place] = zero
            ref[place + length : place + length + PAD] = zero
    g24[...] = jnp.zeros_like(g24)
    p_small[...] = jnp.zeros_like(p_small)
    red.diag(0)
    wait("cs", "cl", "n2t", "wd0", "wd2", "ga0", "ga1", "ua0", "ua1")

    def glu_back(i):
        first, y = tile_start(i)
        slot = lax.rem(i, 2)

        @pl.when(i + 1 < total_tiles)
        def _():
            for which in range(2):
                tile_copy(i + 1, which).start()

        for which in range(2):
            tile_copy(i, which).wait()
        cols = pl.ds(pl.multiple_of(first, BLK), BLK)
        every = pl.ds(pl.multiple_of(y * 2 * half + first, BLK), BLK)
        d_act = dot_nt(cot[...], wd[every, :])
        d_gate = (d_act * apb[slot].astype(f32)).astype(bf16)
        d_up = (d_act * geb[slot].astype(f32)).astype(bf16)
        g96[0:1, every] = jnp.sum(fold(d_gate.astype(f32)), axis=0, keepdims=True)
        g96[1:2, every] = jnp.sum(fold(d_up.astype(f32)), axis=0, keepdims=True)
        for m in range(0, rows, 320):
            acc[m : m + 320] += dot_nt(d_gate[m : m + 320], wg[y, :, cols]) + dot_nt(d_up[m : m + 320], wu[y, :, cols])
        wg[y, :, cols] = dot(n2t[...], d_gate).astype(bf16)
        wu[y, :, cols] = dot(n2t[...], d_up).astype(bf16)

    def tile_range(first, steps):
        def tile(i):
            glu_back(i + first)
            for q, step in steps.items():
                pl.when(i == q)(step)

        loop(per, tile)

    def both(*steps):
        def run():
            for name, k in steps:
                getattr(red, name)(k)

        return run

    tile_range(0, {2: both(("near", 0))})
    red.core(1)
    red.core(2)
    wait("wd1", "wd3", "gb0", "gb1", "ub0", "ub1")
    tile_range(per, {2: both(("diag", 1), ("diag", 2))})
    red.core(3)
    red.core(4)
    red.far(0)
    red.near(1)
    wait("hid", "ga_a", "ga_b")

    def branch_two(i):
        r = rows_at(i, 128)
        value = dot(gpj[r, :], wd[0:wide3, :]) + dot(gm[r, :], wd[wide3:, :])
        gm[r, :] = (big[r, :] + value + v24[10:11, :]).astype(bf16)

    loop(rows // 128, branch_two)
    outs = [
        pltpu.make_async_copy(gm.at[0:short], y_s, out_sem.at[0]),
        pltpu.make_async_copy(gm.at[short:rows], y_l, out_sem.at[1]),
    ]
    for copy in outs:
        copy.start()
    load("proj", r_proj, gpj)
    red.near(2)
    red.diag(3)
    red.diag(4)
    red.last(0)
    for copy in outs:
        copy.wait()

    def norm_two(i):
        r = rows_at(i, 64)
        h, scale = normal(big[r, :])
        d_norm = acc[r, :]
        c = cot[r, :].astype(f32)
        e = d_norm * v24[8:9, :]
        d_hid = c + scale * (e - jnp.mean(e, -1, keepdims=True) - h * jnp.mean(e * h, -1, keepdims=True))
        low = d_hid.astype(bf16)
        acc[r, :] = d_hid
        gm[r, :] = low
        for row, v in ((8, d_norm * h), (9, d_norm), (10, c), (5, low.astype(f32))):
            g24[row : row + 1, :] += jnp.sum(fold(v), axis=0, keepdims=True)

    loop(rows // 64, norm_two)
    red.far(1)
    wait("mixedt", "wo0", "wo1")
    wide = wo.shape[2]

    def out_back(i):
        r = rows_at(i, 128)
        big[r, :] = dot_nt(gm[r, 0:wide], wo[0]) + dot_nt(gm[r, wide : 2 * wide], wo[1])

    loop(rows // 128, out_back)
    for y in range(2):
        wo[y] = dot(mixedt[...], gm[:, y * wide : (y + 1) * wide]).astype(bf16)
    red.core(5)
    load("n1t", r_n1, n2t)
    load("ts", ts, gm.at[0:short])
    load("tl", tl, gm.at[short:rows])
    red.far(2)
    wait("proj", "fs", "fst", "fl", "flt")
    size = shape.chunk

    def mix_back(j, pumps):
        ch = slice(j * BLK, (j + 1) * BLK)
        los = [b * D + j * BLK for b in range(3)]
        tap = [[v72[1 + k : 2 + k, lo : lo + BLK] for k in range(3)] for lo in los]
        ctap = [v24[k : k + 1, ch] for k in range(3)]
        inner, outer = v24[3:4, ch], v24[4:5, ch]
        for copy in block_copies(j):
            copy.wait()

        def spread_out(i):
            here = pl.ds(shape.place(i), size)
            for b in range(3):
                pj[b, here, :] = gpj[shape.plain(i), los[b] : los[b] + BLK].astype(f32)

        def gates(i):
            r, p = shape.plain(i), shape.place(i)
            here = pl.ds(p, size)
            d_mix = big[r, ch]
            rhs[r, :BLK] = (d_mix * taps3(window3(pj.at[0], p, size), tap[0])).astype(bf16)
            dco[here, :] = d_mix * blong[r, :].astype(f32)
            gr[r, :] = taps3(window3(pj.at[1], p, size), tap[1])
            vap[here, :] = taps3(window3(pj.at[2], p, size), tap[2])

        loop(shape.count, spread_out)
        loop(shape.count, gates)

        def conv_down(b):
            def go(i, sums):
                r, p = shape.plain(i), shape.place(i)
                views = window3(dco, p, size)
                low = taps3(views, tap[b], True).astype(bf16)
                gpj[r, los[b] : los[b] + BLK] = low
                parts = [low.astype(f32)] + [views[1] * v for v in window3(pj.at[b], p, size)]
                return tuple(s + fold(v) for s, v in zip(sums, parts))

            sums = lax.fori_loop(0, shape.count, go, (jnp.zeros((8, BLK), f32),) * 4)
            for k in range(4):
                g72[k : k + 1, los[b] : los[b] + BLK] = jnp.sum(sums[k], axis=0, keepdims=True)

        for (start, length, _), table in zip(shape.segs, (s_fs, s_fl)):
            tr[start : start + length] = dot(table[...], rhs[start : start + length, :BLK])
        conv_down(0)
        pumps[0]()

        def filt_back(i, sums):
            a, b = shape.halves(i)
            pa, pb = tr[a, :], tr[b, :]
            sa, sb = bspec[a, :].astype(f32), bspec[b, :].astype(f32)
            ca, cb = bcarr[a, :].astype(f32), bcarr[b, :].astype(f32)
            ta, tb = jnp.tanh(sa * inner), jnp.tanh(sb * inner)
            fa, fb = ta * outer, tb * outer
            first = jnp.logical_and(lax.broadcasted_iota(jnp.int32, pa.shape, 0) == 0, i <= 1)
            pa = jnp.where(first, pa, 2.0 * pa)
            pb = jnp.where(first, pb, 2.0 * pb)
            ra, rb = pa * ca, pb * cb
            ua, ub = pa * fa, pb * fb
            dfa = jnp.where(first, ra, ra + rb)
            dfb = jnp.where(first, rb, pb * ca - pa * cb)
            rhs[a, BLK:] = jnp.where(first, ua, ua + ub).astype(bf16)
            rhs[b, BLK:] = jnp.where(first, ub, pb * fa - pa * fb).astype(bf16)
            dta, dtb = dfa * outer * (1.0 - ta * ta), dfb * outer * (1.0 - tb * tb)
            rhs[a, :BLK] = (dta * inner).astype(bf16)
            rhs[b, :BLK] = (dtb * inner).astype(bf16)
            return sums[0] + fold(dta * sa + dtb * sb), sums[1] + fold(dfa * ta + dfb * tb)

        sums = lax.fori_loop(0, shape.count, filt_back, (jnp.zeros((8, BLK), f32),) * 2)
        for k in range(2):
            g24[3 + k : 4 + k, ch] = jnp.sum(sums[k], axis=0, keepdims=True)
        if j < 2:
            for copy in block_copies(j + 1):
                copy.start()
        for (start, length, place), table in zip(shape.segs, (s_fst, s_flt)):
            dcp[place : place + length] = dot(table[...], rhs[start : start + length, :BLK])
            tr[start : start + length] = dot(table[...], rhs[start : start + length, BLK:])
        pumps[1]()

        def right(i):
            here = pl.ds(shape.place(i), size)
            dco[here, :] = tr[shape.plain(i), :] * vap[here, :]

        loop(shape.count, right)
        conv_down(1)

        def value(i, sums):
            r, p = shape.plain(i), shape.place(i)
            views = window3(dcp, p, size)
            dco[pl.ds(p, size), :] = taps3(views, ctap, True) + tr[r, :] * gr[r, :]
            return tuple(s + fold(views[1] * v) for s, v in zip(sums, window3(vap, p, size)))

        sums = lax.fori_loop(0, shape.count, value, (jnp.zeros((8, BLK), f32),) * 3)
        for k in range(3):
            g24[k : k + 1, ch] = jnp.sum(sums[k], axis=0, keepdims=True)
        conv_down(2)
        pumps[2]()

    none = lambda: None
    mix_back(0, [none, both(("diag", 5)), none])
    mix_back(1, [both(("near", 3)), both(("near", 4)), both(("last", 1))])
    mix_back(2, [both(("last", 2)), none, none])
    wait("n1t", "wi0", "wi1")

    def in_weight(i):
        t, y = i // 2, lax.rem(i, 2)
        cols = pl.ds(pl.multiple_of((3 * y + t) * span, 128), span)
        there = pl.ds(pl.multiple_of(y * span, 128), span)
        wd[rows_at(t, n), there] = dot(n2t[...], gpj[:, cols]).astype(bf16)
        for q, step in IN_STEPS.items():
            pl.when(i == q)(both(*step))

    loop(6, in_weight)
    deep = wi.shape[2]

    def in_back(i):
        r = rows_at(i, 128)
        big[r, :] = dot_nt(gpj[r, 0:deep], wi[0]) + dot_nt(gpj[r, deep : 2 * deep], wi[1])
        for q, step in BACK_STEPS.items():
            pl.when(i == q)(both(*step))

    loop(rows // 128, in_back)
    wait("ts", "tl")

    def norm_one(i):
        r = rows_at(i, 64)
        h, scale = normal(gm[r, :].astype(f32))
        d_norm = big[r, :]
        e = d_norm * v24[6:7, :]
        acc[r, :] += scale * (e - jnp.mean(e, -1, keepdims=True) - h * jnp.mean(e * h, -1, keepdims=True))
        for row, v in ((6, d_norm * h), (7, d_norm)):
            g24[row : row + 1, :] += jnp.sum(fold(v), axis=0, keepdims=True)

    loop(rows // 64, norm_one)
    outs = [
        pltpu.make_async_copy(acc.at[0:short], o_s, out_sem.at[0]),
        pltpu.make_async_copy(acc.at[short:rows], o_l, out_sem.at[1]),
    ]
    for copy in outs:
        copy.start()
    red.far(5)
    red.near(6)
    red.last(3)
    repack(g72, 4, widths[0], 0, p_small)
    red.near(7)
    repack(g24, 11, widths[1], 4, p_small)
    repack(g96, 2, widths[2], 15, p_small)
    red.core(9)
    both(*TAIL_STEPS)()
    for copy in outs:
        copy.wait()
    red.finish()


IN_STEPS = {
    1: (("core", 6), ("near", 5)),
    3: (("core", 7), ("far", 3)),
    5: (("core", 8), ("diag", 6)),
}
BACK_STEPS = {1: (("diag", 7),), 4: (("diag", 8), ("far", 4))}
TAIL_STEPS = (
    ("near", 8), ("last", 4), ("diag", 9), ("far", 6), ("near", 9), ("far", 7), ("far", 8), ("far", 9),
    ("last", 5), ("last", 6), ("last", 7), ("last", 8), ("last", 9),
)


def backward(ts, tl, cs, cl, shards, weights, vecs, res, tables):
    shape = Rows(ts.shape[1], tl.shape[1])
    short, long, rows = shape.short, shape.long, shape.total
    widths = (shards[1].shape[0], shards[6].shape[0], shards[13].shape[1])
    S = jax.ShapeDtypeStruct
    V = pltpu.VMEM
    w_in, w_out, w_gate, w_up, w_down = weights
    n1t, proj, spec, carr, longc, mixedt, hid, n2t, pd, ga, ap, ge = res
    ins = [pd, w_gate, w_up, w_down, w_out, w_in, ts.reshape(short, D), tl.reshape(long, D), cs.reshape(short, D),
           cl.reshape(long, D), vecs[0], vecs[1], n1t, proj, spec, carr, longc, mixedt, hid, n2t, ga, ap, ge]
    ins += list(tables)
    any_ = pl.BlockSpec(memory_space=pl.ANY)
    vm = pl.BlockSpec(memory_space=pltpu.VMEM)
    in_specs = [any_] * 10 + [vm] * 2 + [any_] * 15
    shard = [shards[i].shape for i in LARGE]
    outs = [S((short, D), bf16), S((long, D), bf16), S((short, D), f32), S((long, D), f32)]
    outs += [S(s, f32) for s in shard] + [S((24, 128), f32)]
    half, span = shard[2][1] // 2, shard[0][1] // 3
    dims = [shard[4]] + [(shard[2][0], half)] * 4 + [shard[1]] + [(shard[0][0], span)] * 3 + [(24, 128)]
    kinds = [bf16] * 9 + [f32]
    scratch = []
    for lead in ((8, 2), (2,), (2,), (4,), (4,), (3,)):
        scratch += [V(lead + d, t) for d, t in zip(dims, kinds)]
    wide = lambda s: (2, 16 * s[0], s[1])
    scratch += [
        V((8, 2) + shard[4], bf16), V((16 * shard[4][0], 2 * shard[4][1]), bf16), V(wide(shard[2]), bf16),
        V(wide(shard[3]), bf16), V(wide(shard[1]), bf16), V(wide(shard[0]), bf16), V((2, 384, 128), f32),
        V((rows, D), bf16), V((D, rows), bf16), V((2, rows, BLK), bf16), V((2, rows, BLK), bf16),
        V((rows, D), f32), V((rows, D), f32), V((rows, D), bf16), V((D, rows), bf16), V((rows, 3 * D), bf16),
        V((rows, BLK), bf16), V((rows, BLK), bf16), V((rows, BLK), bf16),
        V((3, shape.padded, BLK), f32), V((shape.padded, BLK), f32), V((shape.padded, BLK), f32),
        V((rows, BLK), f32), V((shape.padded, BLK), f32), V((rows, 2 * BLK), bf16), V((rows, BLK), f32),
    ]
    scratch += [V((m, m), bf16) for m in (short, short, long, long)]
    scratch += [V((8, 32 * widths[0]), f32), V((16, 32 * widths[1]), f32), V((8, 32 * widths[2]), f32)]
    sem = pltpu.SemaphoreType.DMA
    scratch += [sem((10, 31)), sem((10, 23)), sem((8, 2)), sem((36,)), sem((2, 2)), sem((3,)), sem((2,))]
    return pl.pallas_call(
        functools.partial(backward_kernel, shape, widths),
        out_shape=outs,
        in_specs=in_specs,
        out_specs=[any_] * 4 + [vm] * 6,
        scratch_shapes=scratch,
        compiler_params=pltpu.CompilerParams(collective_id=1, has_side_effects=True, vmem_limit_bytes=67043328),
    )(*ins)


def finish_kernel(spans, *refs):
    n = 9
    small, bulk = refs[0], refs[1 : 1 + n]
    outs = refs[1 + n : 1 + 2 * n]
    smalls = refs[1 + 2 * n : 1 + 2 * n + len(spans)]
    bufs = refs[1 + 2 * n + len(spans) : 1 + 3 * n + len(spans)]
    sem = refs[-1]
    ins = [pltpu.make_async_copy(a, b, sem.at[0, k]) for k, (a, b) in enumerate(zip(bulk, bufs))]
    for copy in ins:
        copy.start()
    for (first, count, width), ref in zip(spans, smalls):
        ref[...] = small[first : first + count, 0:width]
    back = [pltpu.make_async_copy(a, b, sem.at[1, k]) for k, (a, b) in enumerate(zip(bufs, outs))]
    for one, two in zip(ins, back):
        one.wait()
        two.start()
    for copy in back:
        copy.wait()


def finish(small, bulk, shards):
    spans = []
    first = 0
    for i in SMALL:
        s = shards[i].shape
        count = s[0] if len(s) == 2 else 1
        spans.append((first, count, s[-1]))
        first += count
    S = jax.ShapeDtypeStruct
    any_ = pl.BlockSpec(memory_space=pl.ANY)
    vm = pl.BlockSpec(memory_space=pltpu.VMEM)
    made = pl.pallas_call(
        functools.partial(finish_kernel, spans),
        out_shape=[S(a.shape, a.dtype) for a in bulk] + [S((c, w), f32) for _, c, w in spans],
        in_specs=[vm] + [any_] * len(bulk),
        out_specs=[any_] * len(bulk) + [vm] * len(spans),
        scratch_shapes=[pltpu.VMEM(a.shape, a.dtype) for a in bulk] + [pltpu.SemaphoreType.DMA((2, len(bulk)))],
    )(small, *bulk)
    grads = {i: v.reshape(shards[i].shape) for i, v in zip(SMALL, made[len(bulk) :])}
    return made[: len(bulk)], grads


def ring_step(ts, tl, cs, cl, shards):
    f = forward(ts, tl, cs, cl, shards)
    b = backward(ts, tl, cs, cl, shards, f[0:5], f[5:8], f[8:20], f[20:24])
    bulk, grads = finish(b[9], b[:9], shards)
    for i, g in zip(LARGE, bulk[4:9]):
        grads[i] = g
    seqs = (ts, tl, ts, tl)
    return tuple(v.reshape(s.shape) for v, s in zip(bulk, seqs)) + tuple(grads[i] for i in range(16))


def table(length):
    half = length // 2
    t = np.arange(length)
    k = np.arange(half)
    ang = 2.0 * np.pi * (np.outer(k, t) % length) / length
    top = np.cos(ang)
    low = -np.sin(ang)
    low[0] = np.where(t % 2 == 0, 1.0, -1.0)
    return (np.concatenate([top, low]) / math.sqrt(length)).astype(np.float32)

def dft(form, tab, v):
    return jnp.einsum(form, jnp.asarray(tab, bf16), v.astype(bf16), preferred_element_type=f32)

def down(v): return jnp.pad(v[:, :-1], ((0,0),(1,0),(0,0)))
def up(v): return jnp.pad(v[:, 1:], ((0,0),(0,1),(0,0)))
def conv(v, k): return k[0]*down(v)+k[1]*v+k[2]*up(v)
def conv_back(g, k): return k[0]*up(g)+k[1]*g+k[2]*down(g)
def conv_kernel(g, v):
    return jnp.stack([jnp.sum(g*down(v),(0,1)), jnp.sum(g*v,(0,1)), jnp.sum(g*up(v),(0,1))])

def weights(length):
    half = length//2
    w = np.full((half,1),2.0,np.float32); w[0]=1.0
    return np.concatenate([w,w])

def mixer_fwd(proj, sk, ck, fg):
    D = ck.shape[1]; L = proj.shape[1]; H=L//2
    tab = table(L); w = weights(L)
    co = conv(proj, sk)
    gl, gr, va = co[:,:,:D], co[:,:,D:2*D], co[:,:,2*D:]
    cond = conv(va, ck)
    spec = dft("kt,btc->bkc", tab, cond)
    carr = dft("kt,btc->bkc", tab, gr*va)
    th = jnp.tanh(spec*fg[0]); filt = th*fg[1]
    first = (lax.broadcasted_iota(jnp.int32,(H,1),0)==0)
    fa, fb, ca, cb = filt[:,:H], filt[:,H:], carr[:,:H], carr[:,H:]
    pa = fa*ca - jnp.where(first,0.0,fb*cb)
    pb = jnp.where(first, fb*cb, fa*cb+fb*ca)
    prod = jnp.concatenate([pa,pb],1)*w
    longc = dft("kt,bkc->btc", tab, prod)
    return gl*longc, (co, spec, th, carr, longc)

def mixer_bwd(dmix, proj, res, sk, ck, fg):
    co, spec, th, carr, longc = res
    D = ck.shape[1]; L = proj.shape[1]; H=L//2
    tab = table(L); w = weights(L)
    gl, gr, va = co[:,:,:D], co[:,:,D:2*D], co[:,:,2*D:]
    dgl = dmix*longc
    dlong = dmix*gl
    dp = dft("kt,btc->bkc", tab, dlong)*w
    filt = th*fg[1]
    first = (lax.broadcasted_iota(jnp.int32,(H,1),0)==0)
    fa, fb, ca, cb = filt[:,:H], filt[:,H:], carr[:,:H], carr[:,H:]
    da, db = dp[:,:H], dp[:,H:]
    dfa = da*ca + jnp.where(first,0.0,db*cb)
    dfb = jnp.where(first, db*cb, db*ca-da*cb)
    dca = da*fa + jnp.where(first,0.0,db*fb)
    dcb = jnp.where(first, db*fb, db*fa-da*fb)
    df = jnp.concatenate([dfa,dfb],1); dc = jnp.concatenate([dca,dcb],1)
    dth = df*fg[1]*(1-th*th)
    dfg = jnp.stack([jnp.sum(dth*spec,(0,1)), jnp.sum(df*th,(0,1))])
    dcond = dft("kt,bkc->btc", tab, dth*fg[0])
    dgv = dft("kt,bkc->btc", tab, dc)
    dck = conv_kernel(dcond, va)
    dva = conv_back(dcond, ck) + dgv*gr
    dgr = dgv*va
    dco = jnp.concatenate([dgl,dgr,dva],2)
    dsk = conv_kernel(dco, proj)
    return conv_back(dco, sk), dsk, dck, dfg

def mm(a,b): return jnp.dot(a,b,preferred_element_type=f32)
def tn(a,b): return lax.dot_general(a,b,(((0,),(0,)),((),())),preferred_element_type=f32)
def nt(a,b): return lax.dot_general(a,b,(((1,),(1,)),((),())),preferred_element_type=f32)

def norm(v):
    m = jnp.mean(v,-1,keepdims=True); d = v-m
    r = lax.rsqrt(jnp.mean(d*d,-1,keepdims=True)+1e-5)
    return d*r, r

def norm_back(e, h, r):
    return r*(e-jnp.mean(e,-1,keepdims=True)-h*jnp.mean(e*h,-1,keepdims=True))

C0=math.sqrt(2/math.pi); C1=0.044715
def gelu_parts(g):
    t = jnp.tanh(C0*(g+C1*g*g*g))
    return 0.5*g*(1+t), 0.5*(1+t)+0.5*g*(1-t*t)*C0*(1+3*C1*g*g)

def local(ts, tl, P, cs, cl):
    (iw, ib, sk, ck, fg, ow, ob, g1, b1, g2, b2, gw, uw, gb, dw, db) = [p if i in (0,5,11,12,14) else p.astype(f32) for i,p in enumerate(P)]
    D = ow.shape[0]
    ns = ts.shape[0]*ts.shape[1]
    x = jnp.concatenate([ts.reshape(-1,D),tl.reshape(-1,D)]).astype(f32)
    c = jnp.concatenate([cs.reshape(-1,D),cl.reshape(-1,D)])
    h1, r1 = norm(x)
    n1 = (h1*g1+b1).astype(bf16)
    proj = mm(n1, iw)+ib
    ps, pl_ = proj[:ns].reshape(ts.shape[0],ts.shape[1],3*D), proj[ns:].reshape(tl.shape[0],tl.shape[1],3*D)
    ms, rs = mixer_fwd(ps, sk, ck, fg); ml, rl = mixer_fwd(pl_, sk, ck, fg)
    mixed = jnp.concatenate([ms.reshape(-1,D),ml.reshape(-1,D)]).astype(bf16)
    hid = x + mm(mixed, ow)+ob
    h2, r2 = norm(hid)
    n2 = (h2*g2+b2).astype(bf16)
    gp = mm(n2,gw)+gb[0]; up_ = mm(n2,uw)+gb[1]
    ge, gd = gelu_parts(gp)
    ga = (ge*up_).astype(bf16)
    out = (hid+mm(ga,dw)+db).astype(bf16)
    cf = c.astype(f32)
    d_db = jnp.sum(cf,0); d_dw = tn(ga,c)
    dg = nt(c,dw)
    dgate = (dg*up_*gd).astype(bf16); dup=(dg*ge).astype(bf16)
    d_gb = jnp.stack([jnp.sum(dgate.astype(f32),0),jnp.sum(dup.astype(f32),0)])
    d_gw = tn(n2,dgate); d_uw = tn(n2,dup)
    dn2 = nt(dgate,gw)+nt(dup,uw)
    d_g2 = jnp.sum(dn2*h2,0); d_b2=jnp.sum(dn2,0)
    dh = cf + norm_back(dn2*g2,h2,r2)
    gm = dh.astype(bf16)
    d_ob = jnp.sum(gm.astype(f32),0); d_ow = tn(mixed,gm)
    dm = nt(gm,ow)
    dps, a1,a2,a3 = mixer_bwd(dm[:ns].reshape(ts.shape), ps, rs, sk, ck, fg)
    dpl, e1,e2,e3 = mixer_bwd(dm[ns:].reshape(tl.shape), pl_, rl, sk, ck, fg)
    gpj = jnp.concatenate([dps.reshape(-1,3*D),dpl.reshape(-1,3*D)]).astype(bf16)
    d_ib = jnp.sum(gpj.astype(f32),0); d_iw = tn(n1,gpj)
    dn1 = nt(gpj,iw)
    d_g1=jnp.sum(dn1*h1,0); d_b1=jnp.sum(dn1,0)
    dx = dh + norm_back(dn1*g1,h1,r1)
    return (out[:ns].reshape(ts.shape), out[ns:].reshape(tl.shape), dx[:ns].reshape(ts.shape), dx[ns:].reshape(tl.shape),
        d_iw,d_ib,a1+e1,a2+e2,a3+e3,d_ow,d_ob,d_g1,d_b1,d_g2,d_b2,d_gw,d_uw,d_gb,d_dw,d_db)


def fetch_plain(shards):
    params = []
    for i, shard in enumerate(shards):
        if i in LARGE:
            wide = lax.all_gather(shard, "narrow", axis=1, tiled=True)
            params.append(lax.all_gather(wide, "wide", axis=0, tiled=True))
        else:
            params.append(
                lax.all_gather(shard, ("wide", "narrow"), axis=shard.ndim - 1, tiled=True)
            )
    return params


def reduce_plain(grads, shards):
    outs = []
    for i, grad in enumerate(grads):
        if i in LARGE:
            block = lax.psum_scatter(grad.astype(bf16), "wide", scatter_dimension=0, tiled=True)
            block = lax.psum_scatter(block, "narrow", scatter_dimension=1, tiled=True)
            outs.append(block.astype(f32))
        else:
            outs.append(
                lax.psum_scatter(
                    grad, ("wide", "narrow"), scatter_dimension=grad.ndim - 1, tiled=True
                )
            )
    return outs


def plain_step(ts, tl, cs, cl, shards):
    results = local(ts, tl, fetch_plain(shards), cs, cl)
    return tuple(results[:4]) + tuple(reduce_plain(results[4:], shards))


def body(ring, ts, tl, *rest):
    step = ring_step if ring and ts.shape[0] == 1 and tl.shape[0] == 1 else plain_step
    return step(ts, tl, rest[16], rest[17], list(rest[:16]))


def solution(mesh):
    ring = mesh.shape["wide"] == 16 and mesh.shape["narrow"] == 2
    seq = P(("wide", "narrow"), None, None)
    mat = P("wide", "narrow")
    vec = P(("wide", "narrow"))
    pair = P(None, ("wide", "narrow"))
    params = (mat, vec, pair, pair, pair, mat, vec, vec, vec, vec, vec, mat, mat, pair, mat, vec)
    return jax.shard_map(
        functools.partial(body, ring),
        mesh=mesh,
        in_specs=(seq, seq) + params + (seq, seq),
        out_specs=(seq, seq, seq, seq) + params,
        check_vma=False,
    )
```

profile of v0, /device:TPU:0, one launch (start us, length us, event | category | flops | bytes accessed | tf_op | source)
XLA Modules:
  0.0 230.4 jit_solution(18342209044087880162)
XLA Ops:
  0.7 1.4 pad_add_fusion.refs_0_
  2.1 106.4 %shard_map.365 = (bf16[768,2304]{1,0:T(8,128)(2,1)}, bf16[768,768]{1,0:T(8,128)(2,1)}, bf16[768,3072]{1,0:T(8,128)(2,1)}, bf16[768,3072]{1,0:T(8,128)(2,1)}, bf1...) custom-call(bf16[32,128]{1,0:T(8,128)(2,1)} %pad_add_fusion.refs_0_,, ...), custom_call_target="tpu_custom_call" | custom-call | tf_op jit(solution)/shard_map/pallas_call | solution.py:560
  108.5 116.8 %shard_map.366 = (bf16[128,768]{1,0:T(8,128)(2,1)}, bf16[512,768]{1,0:T(8,128)(2,1)}, f32[128,768]{1,0:T(8,128)}, f32[512,768]{1,0:T(8,128)}, f32[48,1152]{1,0:T...) custom-call(bf16[3072,768]{1,0:T(8,128)(2,1)} %get-tuple-element.73., ...), custom_call_target="tpu_custom_call" | custom-call | tf_op jit(solution)/shard_map/pallas_call | solution.py:1120
  225.3 4.9 %shard_map.367 = (bf16[128,768]{1,0:T(8,128)(2,1)}, bf16[512,768]{1,0:T(8,128)(2,1)}, f32[128,768]{1,0:T(8,128)}, f32[512,768]{1,0:T(8,128)}, f32[48,1152]{1,0:T...) custom-call(f32[24,128]{1,0:T(8,128)} %get-tuple-element.96.refs_0_,, ...), custom_call_target="tpu_custom_call" | custom-call | tf_op jit(solution)/shard_map/pallas_call | solution.py:1161
where the time goes:
time: 231 us; the launch traced here: 230 us
  Pallas kernels  228 us (99%)
    pallas_call x1, Pallas kernels, backward(): pl.pallas_call(functools.partial(backward_kernel, shape, widths), out_sha...  117 us
    pallas_call x1, Pallas kernels, forward(): pl.pallas_call(functools.partial(forward_kernel, shape, widths), out_shap...  106 us
    pallas_call x1, Pallas kernels, finish(): pl.pallas_call(functools.partial(finish_kernel, spans), out_shape=[S(a.sh...  4.92 us

commit v1 on v0

--- a/solution.py
+++ b/solution.py
@@ -25,12 +25,6 @@
 
 def flat(z, x, c):
     return (z * 2 + x) * 2 + c
-
-
-def window(ref, rows, cols, w, y):
-    return ref.at[
-        pl.ds(pl.multiple_of(w * rows, 16), rows), pl.ds(pl.multiple_of(y * cols, 128), cols)
-    ]
 
 
 def greet(peers):
@@ -294,10 +288,10 @@
 def forward_kernel(shape, widths, *refs):
     (pack, w0, w1, w2, w3, w4, ts, tl, cs, cl, ps, pl_) = refs[:12]
     (g_in, g_out, g_gate, g_up, g_down, v72, v24, v96, o_n1, o_proj, o_spec, o_carr, o_long,
-     o_mixed, o_hid, o_n2, o_pd, o_ga, o_ap, o_ge, o_fs, o_fst, o_fl, o_flt) = refs[12:36]
+     o_mixed, o_hid, o_n2, o_pd, o_ga, o_ap, o_ge, o_fs, o_fst, o_fl, o_flt, o_gl, o_gr, o_va) = refs[12:39]
     (f_small, f_in, f_out, f_gate, f_up, smallw, x, cot, n1, n1t, proj, spec, carr, longc,
-     mixed, mixedt, hid, n2, n2t, ga, ap, ge, pd, pj, gl, vap, rhs, tr, prod, s_ps, s_pl, s_fs, s_fst,
-     s_fl, s_flt, ici_send, ici_recv, core_send, core_recv, own_sem, load_sem, save_sem) = refs[36:]
+     mixed, mixedt, hid, n2, n2t, ga, ap, ge, pd, pj, gl, vap, rhs, tr, prod, lows, s_ps, s_pl, s_fs, s_fst,
+     s_fl, s_flt, ici_send, ici_recv, core_send, core_recv, own_sem, load_sem, save_sem) = refs[39:]
     rows = shape.total
     short = shape.short
     zp, xp, yp, cp = neighbours()
@@ -386,10 +380,14 @@
         def convolve(i):
             r, p = shape.plain(i), shape.place(i)
             here = pl.ds(p, n)
-            gl[r, :] = taps3(window3(pj.at[0], p, n), tap[0])
+            left = taps3(window3(pj.at[0], p, n), tap[0])
+            right = taps3(window3(pj.at[1], p, n), tap[1])
             value = taps3(window3(pj.at[2], p, n), tap[2])
+            gl[r, :] = left
             vap[here, :] = value
-            rhs[r, BLK:] = (taps3(window3(pj.at[1], p, n), tap[1]) * value).astype(bf16)
+            rhs[r, BLK:] = (right * value).astype(bf16)
+            for q, v in enumerate((left, right, value)):
+                lows[q, r, ch] = v.astype(bf16)
 
         def condition(i):
             rhs[shape.plain(i), :BLK] = taps3(window3(vap, shape.place(i), n), ctap).astype(bf16)
@@ -427,6 +425,8 @@
         mix(j, MIX_PUMPS[j])
     for a, b in ((proj, o_proj), (spec, o_spec), (carr, o_carr), (longc, o_long)):
         save(a, b)
+    for q, b in enumerate((o_gl, o_gr, o_va)):
+        save(lows.at[q], b)
     pump(3)
     mixedt[...] = mixed[...].T
     save(mixedt, o_mixed)
@@ -445,51 +445,56 @@
     n2t[...] = n2[...].T
     save(n2t, o_n2)
 
-    def glu(i):
+    def gate_half(i):
         cols = rows_at(i, BLK)
         for m in range(0, rows, 320):
             gate = dot(n2[m : m + 320, :], f_gate[:, cols]) + v96[0:1, cols]
-            up = dot(n2[m : m + 320, :], f_up[:, cols]) + v96[1:2, cols]
             square = gate * gate
             t = jnp.tanh(gate * (GELU_A + GELU_A * GELU_B * square))
             half = 0.5 * (1.0 + t)
-            act = gate * half
             slope = half + 0.5 * gate * (1.0 - t * t) * (GELU_A + 3.0 * GELU_A * GELU_B * square)
-            ga[m : m + 320, cols] = (act * up).astype(bf16)
-            ge[m : m + 320, cols] = act.astype(bf16)
-            ap[m : m + 320, cols] = (up * slope).astype(bf16)
+            ge[m : m + 320, cols] = (gate * half).astype(bf16)
+            ap[m : m + 320, cols] = slope.astype(bf16)
+
+    def up_half(i):
+        cols = rows_at(i, BLK)
+        for m in range(0, rows, 320):
+            up = dot(n2[m : m + 320, :], f_up[:, cols]) + v96[1:2, cols]
+            ga[m : m + 320, cols] = (ge[m : m + 320, cols].astype(f32) * up).astype(bf16)
+            ap[m : m + 320, cols] = (ap[m : m + 320, cols].astype(f32) * up).astype(bf16)
         pd[cols, :] = dot(ga[:, cols].T, cot[...]).astype(bf16)
+
+    def pairs(part):
+        return [(ga.at[:, part], o_ga.at[:, part]), (ap.at[:, part], o_ap.at[:, part]), (pd.at[part], o_pd.at[part])]
+
+    def save_first():
+        for k, (a, b) in enumerate(pairs(slice(0, pd.shape[0] // 2))):
+            pltpu.make_async_copy(a, b, load_sem.at[k]).start()
+
+    tiles = ga.shape[1] // BLK
+
+    def staged(fn, counts, more):
+        def tile(i):
+            fn(i)
+            for q, n in enumerate(counts):
+                if n:
+                    pl.when(i == q)(functools.partial(pump, n))
+            if more:
+                pl.when(i == tiles // 2 - 1)(save_first)
+
+        loop(tiles, tile)
 
     need(3)
     save(f_gate, g_gate)
+    staged(gate_half, GATE_PUMPS, False)
+    save(ge, o_ge)
     need(4)
     save(f_up, g_up)
-    tiles = ga.shape[1] // BLK
-
-    def tile(i):
-        glu(i)
-        for q, n in enumerate(GLU_PUMPS):
-            if n:
-                pl.when(i == q)(functools.partial(pump, n))
-        pl.when(i == tiles // 2 - 1)(save_first)
-
-    def save_first():
-        half = pd.shape[0] // 2
-        first = slice(0, half)
-        pairs = [(a.at[:, first], b.at[:, first]) for a, b in ((ga, o_ga), (ap, o_ap), (ge, o_ge))]
-        for k, (a, b) in enumerate(pairs + [(pd.at[first], o_pd.at[first])]):
-            pltpu.make_async_copy(a, b, load_sem.at[k]).start()
-
-    loop(tiles, tile)
+    staged(up_half, UP_PUMPS, True)
     half = pd.shape[0] // 2
-    rest = slice(half, 2 * half)
-    for a, b in ((ga, o_ga), (ap, o_ap), (ge, o_ge)):
-        save(a.at[:, rest], b.at[:, rest])
-    save(pd.at[rest], o_pd.at[rest])
-    first = slice(0, half)
-    early = [(a.at[:, first], b.at[:, first]) for a, b in ((ga, o_ga), (ap, o_ap), (ge, o_ge))]
-    early.append((pd.at[first], o_pd.at[first]))
-    for k, (a, b) in enumerate(early):
+    for a, b in pairs(slice(half, 2 * half)):
+        save(a, b)
+    for k, (a, b) in enumerate(pairs(slice(0, half))):
         pltpu.make_async_copy(a, b, load_sem.at[k]).wait()
     need(5)
     for copy in saves:
@@ -498,13 +503,14 @@
 
 
 GATHER_ORDER = (
-    ("S", 0), ("S", 1), ("S", 2), ("z", 0), ("z", 1), ("p", 0), ("S", 3), ("d", 0), ("z", 2), ("p", 1), ("d", 1),
+    ("S", 0), ("S", 1), ("S", 2), ("S", 3), ("z", 0), ("z", 1), ("p", 0), ("d", 0), ("z", 2), ("p", 1), ("d", 1),
     ("z", 3), ("p", 2), ("S", 4), ("d", 2), ("p", 3), ("z", 4), ("S", 5), ("d", 3), ("p", 4), ("z", 5), ("d", 4),
     ("p", 5), ("d", 5),
 )
-GATHER_FIRST = 3
+GATHER_FIRST = 4
 MIX_PUMPS = ((3, 3, 3), (4, 4, 4), (5, 5, 5))
-GLU_PUMPS = (0, 2, 0, 2, 0, 2, 0, 2, 0, 2, 0, 2)
+GATE_PUMPS = (0, 2, 0, 2, 0, 2, 0, 2, 0, 2, 0, 2)
+UP_PUMPS = (0, 2, 0, 2, 0, 2, 0, 2, 0, 2, 0, 2)
 
 
 def place_rows(piece, first):
@@ -544,7 +550,7 @@
     outs = [S(s, bf16) for s in full] + [S(s, f32) for s in vecs]
     outs += [S((D, rows), bf16), S((rows, 3 * D), bf16)] + [S((rows, D), bf16)] * 3
     outs += [S((D, rows), bf16), S((rows, D), f32), S((D, rows), bf16), S((ff, D), bf16)]
-    outs += [S((rows, ff), bf16)] * 3 + [S(s, bf16) for s in square]
+    outs += [S((rows, ff), bf16)] * 3 + [S(s, bf16) for s in square] + [S((rows, D), bf16)] * 3
     any_ = pl.BlockSpec(memory_space=pl.ANY)
     vm = pl.BlockSpec(memory_space=pltpu.VMEM)
     sem = pltpu.SemaphoreType.DMA
@@ -554,14 +560,14 @@
     scratch += [V((D, rows), bf16), V((rows, D), f32), V((rows, D), bf16), V((D, rows), bf16)]
     scratch += [V((rows, ff), bf16)] * 3 + [V((ff, D), bf16)]
     scratch += [V((3, shape.padded, BLK), f32), V((rows, BLK), f32), V((shape.padded, BLK), f32)]
-    scratch += [V((rows, 2 * BLK), bf16), V((rows, 2 * BLK), f32), V((rows, BLK), bf16)]
+    scratch += [V((rows, 2 * BLK), bf16), V((rows, 2 * BLK), f32), V((rows, BLK), bf16), V((3, rows, D), bf16)]
     scratch += [V(a.shape, f32) for a in angles] + [V(s, bf16) for s in square]
     scratch += [sem((6, 15)), sem((6, 16)), sem((6, 16)), sem((6, 16)), sem((6,)), sem((6,)), sem((28,))]
     return pl.pallas_call(
         functools.partial(forward_kernel, shape, widths),
         out_shape=outs,
         in_specs=[any_] * len(ins),
-        out_specs=[any_] * 5 + [vm] * 3 + [any_] * 16,
+        out_specs=[any_] * 5 + [vm] * 3 + [any_] * 19,
         scratch_shapes=scratch,
         compiler_params=pltpu.CompilerParams(collective_id=0, has_side_effects=True, vmem_limit_bytes=67043328),
     )(*ins)
@@ -705,13 +711,13 @@
 
 def backward_kernel(shape, widths, *refs):
     (pd, h_g, h_u, h_d, h_o, h_i, ts, tl, cs, cl, v72, v24, r_n1, r_proj, r_spec, r_carr, r_long,
-     r_mixed, r_hid, r_n2, r_ga, r_ap, r_ge, fs, fst, fl, flt) = refs[:27]
-    y_s, y_l, o_s, o_l, o_in, o_out, o_gate, o_up, o_down, o_small = refs[27:37]
+     r_mixed, r_hid, r_n2, r_ga, r_ap, r_ge, fs, fst, fl, flt, r_gl, r_gr, r_va) = refs[:30]
+    y_s, y_l, o_s, o_l, o_in, o_out, o_gate, o_up, o_down, o_small = refs[30:40]
     nitem = 10
-    groups = [refs[37 + q * nitem : 37 + (q + 1) * nitem] for q in range(6)]
-    (held, wd, wg, wu, wo, wi, p_small, cot, n2t, apb, geb, acc, big, gm, mixedt, gpj, bspec, bcarr, blong,
-     pj, dco, vap, gr, dcp, rhs, tr, s_fs, s_fst, s_fl, s_flt, g72, g24, g96,
-     send_sem, recv_sem, own_sem, load_sem, tile_sem, blk_sem, out_sem) = refs[37 + 6 * nitem :]
+    groups = [refs[40 + q * nitem : 40 + (q + 1) * nitem] for q in range(6)]
+    (held, wd, wg, wu, wo, wi, p_small, cot, n2t, apb, geb, acc, big, gm, mixedt, gpj, bspec, bcarr, blong, bgl, bgr, bva,
+     dco, dcp, rhs, tr, s_fs, s_fst, s_fl, s_flt, g72, g24, g96,
+     send_sem, recv_sem, own_sem, load_sem, tile_sem, blk_sem, out_sem) = refs[40 + 6 * nitem :]
     rows, short = shape.total, shape.short
     zp, xp, yp, cp = neighbours()
     greet(zp + [xp, yp, cp])
@@ -795,19 +801,20 @@
     for name, a, b in (("fs", fs, s_fs), ("fst", fst, s_fst), ("fl", fl, s_fl), ("flt", flt, s_flt)):
         load(name, a, b)
 
-    def block_copies(j):
+    blocks = ((r_spec, bspec), (r_carr, bcarr), (r_long, blong), (r_gl, bgl), (r_gr, bgr), (r_va, bva))
+
+    def block_copies(j, first, last):
         ch = slice(j * BLK, (j + 1) * BLK)
         return [
-            pltpu.make_async_copy(src.at[:, ch], dst, blk_sem.at[k])
-            for k, (src, dst) in enumerate(((r_spec, bspec), (r_carr, bcarr), (r_long, blong)))
+            pltpu.make_async_copy(blocks[k][0].at[:, ch], blocks[k][1], blk_sem.at[k]) for k in range(first, last)
         ]
 
-    for copy in block_copies(0):
+    for copy in block_copies(0, 0, 6):
         copy.start()
     acc[...] = jnp.zeros_like(acc)
     zero = jnp.zeros((PAD, BLK), f32)
     for start, length, place in shape.segs:
-        for ref in (pj.at[0], pj.at[1], pj.at[2], dco, vap, dcp):
+        for ref in (dco, dcp):
             ref[place - PAD : place] = zero
             ref[place + length : place + length + PAD] = zero
     g24[...] = jnp.zeros_like(g24)
@@ -880,7 +887,6 @@
     red.near(2)
     red.diag(3)
     red.diag(4)
-    red.last(0)
     for copy in outs:
         copy.wait()
 
@@ -898,7 +904,6 @@
             g24[row : row + 1, :] += jnp.sum(fold(v), axis=0, keepdims=True)
 
     loop(rows // 64, norm_two)
-    red.far(1)
     wait("mixedt", "wo0", "wo1")
     wide = wo.shape[2]
 
@@ -913,7 +918,7 @@
     load("n1t", r_n1, n2t)
     load("ts", ts, gm.at[0:short])
     load("tl", tl, gm.at[short:rows])
-    red.far(2)
+    red.far(1)
     wait("proj", "fs", "fst", "fl", "flt")
     size = shape.chunk
 
@@ -923,24 +928,15 @@
         tap = [[v72[1 + k : 2 + k, lo : lo + BLK] for k in range(3)] for lo in los]
         ctap = [v24[k : k + 1, ch] for k in range(3)]
         inner, outer = v24[3:4, ch], v24[4:5, ch]
-        for copy in block_copies(j):
+        for copy in block_copies(j, 0, 4):
             copy.wait()
 
-        def spread_out(i):
-            here = pl.ds(shape.place(i), size)
-            for b in range(3):
-                pj[b, here, :] = gpj[shape.plain(i), los[b] : los[b] + BLK].astype(f32)
-
         def gates(i):
-            r, p = shape.plain(i), shape.place(i)
-            here = pl.ds(p, size)
+            r = shape.plain(i)
             d_mix = big[r, ch]
-            rhs[r, :BLK] = (d_mix * taps3(window3(pj.at[0], p, size), tap[0])).astype(bf16)
-            dco[here, :] = d_mix * blong[r, :].astype(f32)
-            gr[r, :] = taps3(window3(pj.at[1], p, size), tap[1])
-            vap[here, :] = taps3(window3(pj.at[2], p, size), tap[2])
-
-        loop(shape.count, spread_out)
+            rhs[r, :BLK] = (d_mix * bgl[r, :].astype(f32)).astype(bf16)
+            dco[pl.ds(shape.place(i), size), :] = d_mix * blong[r, :].astype(f32)
+
         loop(shape.count, gates)
 
         def conv_down(b):
@@ -948,8 +944,9 @@
                 r, p = shape.plain(i), shape.place(i)
                 views = window3(dco, p, size)
                 low = taps3(views, tap[b], True).astype(bf16)
+                given = gpj[r, los[b] : los[b] + BLK].astype(f32)
                 gpj[r, los[b] : los[b] + BLK] = low
-                parts = [low.astype(f32)] + [views[1] * v for v in window3(pj.at[b], p, size)]
+                parts = [low.astype(f32)] + [views[2 - k] * given for k in range(3)]
                 return tuple(s + fold(v) for s, v in zip(sums, parts))
 
             sums = lax.fori_loop(0, shape.count, go, (jnp.zeros((8, BLK), f32),) * 4)
@@ -986,8 +983,10 @@
         for k in range(2):
             g24[3 + k : 4 + k, ch] = jnp.sum(sums[k], axis=0, keepdims=True)
         if j < 2:
-            for copy in block_copies(j + 1):
+            for copy in block_copies(j + 1, 0, 4):
                 copy.start()
+        for copy in block_copies(j, 4, 6):
+            copy.wait()
         for (start, length, place), table in zip(shape.segs, (s_fst, s_flt)):
             dcp[place : place + length] = dot(table[...], rhs[start : start + length, :BLK])
             tr[start : start + length] = dot(table[...], rhs[start : start + length, BLK:])
@@ -995,7 +994,8 @@
 
         def right(i):
             here = pl.ds(shape.place(i), size)
-            dco[here, :] = tr[shape.plain(i), :] * vap[here, :]
+            r = shape.plain(i)
+            dco[here, :] = tr[r, :] * bva[r, :].astype(f32)
 
         loop(shape.count, right)
         conv_down(1)
@@ -1003,19 +1003,23 @@
         def value(i, sums):
             r, p = shape.plain(i), shape.place(i)
             views = window3(dcp, p, size)
-            dco[pl.ds(p, size), :] = taps3(views, ctap, True) + tr[r, :] * gr[r, :]
-            return tuple(s + fold(views[1] * v) for s, v in zip(sums, window3(vap, p, size)))
+            dco[pl.ds(p, size), :] = taps3(views, ctap, True) + tr[r, :] * bgr[r, :].astype(f32)
+            given = bva[r, :].astype(f32)
+            return tuple(s + fold(views[2 - k] * given) for k, s in enumerate(sums))
 
         sums = lax.fori_loop(0, shape.count, value, (jnp.zeros((8, BLK), f32),) * 3)
         for k in range(3):
             g24[k : k + 1, ch] = jnp.sum(sums[k], axis=0, keepdims=True)
+        if j < 2:
+            for copy in block_copies(j + 1, 4, 6):
+                copy.start()
         conv_down(2)
         pumps[2]()
 
     none = lambda: None
-    mix_back(0, [none, both(("diag", 5)), none])
-    mix_back(1, [both(("near", 3)), both(("near", 4)), both(("last", 1))])
-    mix_back(2, [both(("last", 2)), none, none])
+    mix_back(0, [none, both(("diag", 5)), both(("far", 2))])
+    mix_back(1, [both(("near", 3)), both(("near", 4)), none])
+    mix_back(2, [none, none, none])
     wait("n1t", "wi0", "wi1")
 
     def in_weight(i):
@@ -1056,7 +1060,6 @@
         copy.start()
     red.far(5)
     red.near(6)
-    red.last(3)
     repack(g72, 4, widths[0], 0, p_small)
     red.near(7)
     repack(g24, 11, widths[1], 4, p_small)
@@ -1075,8 +1078,8 @@
 }
 BACK_STEPS = {1: (("diag", 7),), 4: (("diag", 8), ("far", 4))}
 TAIL_STEPS = (
-    ("near", 8), ("last", 4), ("diag", 9), ("far", 6), ("near", 9), ("far", 7), ("far", 8), ("far", 9),
-    ("last", 5), ("last", 6), ("last", 7), ("last", 8), ("last", 9),
+    ("near", 8), ("diag", 9), ("far", 6), ("near", 9), ("far", 7), ("far", 8), ("far", 9),
+    ("last", 0), ("last", 1), ("last", 2), ("last", 3), ("last", 4), ("last", 5), ("last", 6), ("last", 7), ("last", 8), ("last", 9),
 )
 
 
@@ -1087,13 +1090,13 @@
     S = jax.ShapeDtypeStruct
     V = pltpu.VMEM
     w_in, w_out, w_gate, w_up, w_down = weights
-    n1t, proj, spec, carr, longc, mixedt, hid, n2t, pd, ga, ap, ge = res
+    n1t, proj, spec, carr, longc, mixedt, hid, n2t, pd, ga, ap, ge = res[:12]
     ins = [pd, w_gate, w_up, w_down, w_out, w_in, ts.reshape(short, D), tl.reshape(long, D), cs.reshape(short, D),
            cl.reshape(long, D), vecs[0], vecs[1], n1t, proj, spec, carr, longc, mixedt, hid, n2t, ga, ap, ge]
-    ins += list(tables)
+    ins += list(tables) + list(res[12:])
     any_ = pl.BlockSpec(memory_space=pl.ANY)
     vm = pl.BlockSpec(memory_space=pltpu.VMEM)
-    in_specs = [any_] * 10 + [vm] * 2 + [any_] * 15
+    in_specs = [any_] * 10 + [vm] * 2 + [any_] * 18
     shard = [shards[i].shape for i in LARGE]
     outs = [S((short, D), bf16), S((long, D), bf16), S((short, D), f32), S((long, D), f32)]
     outs += [S(s, f32) for s in shard] + [S((24, 128), f32)]
@@ -1109,14 +1112,13 @@
         V(wide(shard[3]), bf16), V(wide(shard[1]), bf16), V(wide(shard[0]), bf16), V((2, 384, 128), f32),
         V((rows, D), bf16), V((D, rows), bf16), V((2, rows, BLK), bf16), V((2, rows, BLK), bf16),
         V((rows, D), f32), V((rows, D), f32), V((rows, D), bf16), V((D, rows), bf16), V((rows, 3 * D), bf16),
-        V((rows, BLK), bf16), V((rows, BLK), bf16), V((rows, BLK), bf16),
-        V((3, shape.padded, BLK), f32), V((shape.padded, BLK), f32), V((shape.padded, BLK), f32),
-        V((rows, BLK), f32), V((shape.padded, BLK), f32), V((rows, 2 * BLK), bf16), V((rows, BLK), f32),
+        *[V((rows, BLK), bf16)] * 6, V((shape.padded, BLK), f32), V((shape.padded, BLK), f32),
+        V((rows, 2 * BLK), bf16), V((rows, BLK), f32),
     ]
     scratch += [V((m, m), bf16) for m in (short, short, long, long)]
     scratch += [V((8, 32 * widths[0]), f32), V((16, 32 * widths[1]), f32), V((8, 32 * widths[2]), f32)]
     sem = pltpu.SemaphoreType.DMA
-    scratch += [sem((10, 31)), sem((10, 23)), sem((8, 2)), sem((36,)), sem((2, 2)), sem((3,)), sem((2,))]
+    scratch += [sem((10, 31)), sem((10, 23)), sem((8, 2)), sem((36,)), sem((2, 2)), sem((6,)), sem((2,))]
     return pl.pallas_call(
         functools.partial(backward_kernel, shape, widths),
         out_shape=outs,
@@ -1171,7 +1173,7 @@
 
 def ring_step(ts, tl, cs, cl, shards):
     f = forward(ts, tl, cs, cl, shards)
-    b = backward(ts, tl, cs, cl, shards, f[0:5], f[5:8], f[8:20], f[20:24])
+    b = backward(ts, tl, cs, cl, shards, f[0:5], f[5:8], f[8:20] + f[24:27], f[20:24])
     bulk, grads = finish(b[9], b[:9], shards)
     for i, g in zip(LARGE, bulk[4:9]):
         grads[i] = g

time: 231 us -> 222 us (0.961)
  Pallas kernels: 228 us -> 220 us
    pallas_call x1, Pallas kernels: 117 us -> 106 us  [backward(): pl.pallas_call(functools.partial(backward_kernel, shape, widths), out_sha...]
    pallas_call x1, Pallas kernels: 106 us -> 109 us  [forward(): pl.pallas_call(functools.partial(forward_kernel, shape, widths), out_shap...]
where the time goes in v1:
time: 222 us
  Pallas kernels  220 us (99%)
    pallas_call x1, Pallas kernels, forward(): pl.pallas_call(functools.partial(forward_kernel, shape, widths), out_shap...  109 us
    pallas_call x1, Pallas kernels, backward(): pl.pallas_call(functools.partial(backward_kernel, shape, widths), out_sha...  106 us
    pallas_call x1, Pallas kernels, finish(): pl.pallas_call(functools.partial(finish_kernel, spans), out_shape=[S(a.sh...  4.92 us

profile of v1, /device:TPU:0, one launch (start us, length us, event | category | flops | bytes accessed | tf_op | source)
XLA Modules:
  0.0 222.2 jit_solution(12583208063746507794)
XLA Ops:
  0.7 1.4 pad_add_fusion.refs_0_
  2.1 109.1 %shard_map.365 = (bf16[768,2304]{1,0:T(8,128)(2,1)}, bf16[768,768]{1,0:T(8,128)(2,1)}, bf16[768,3072]{1,0:T(8,128)(2,1)}, bf16[768,3072]{1,0:T(8,128)(2,1)}, bf1...) custom-call(bf16[32,128]{1,0:T(8,128)(2,1)} %pad_add_fusion.refs_0_,, ...), custom_call_target="tpu_custom_call" | custom-call | tf_op jit(solution)/shard_map/pallas_call | solution.py:566
  111.2 105.9 %shard_map.366 = (bf16[128,768]{1,0:T(8,128)(2,1)}, bf16[512,768]{1,0:T(8,128)(2,1)}, f32[128,768]{1,0:T(8,128)}, f32[512,768]{1,0:T(8,128)}, f32[48,1152]{1,0:T...) custom-call(bf16[3072,768]{1,0:T(8,128)(2,1)} %get-tuple-element.76., ...), custom_call_target="tpu_custom_call" | custom-call | tf_op jit(solution)/shard_map/pallas_call | solution.py:1122
  217.1 4.9 %shard_map.367 = (bf16[128,768]{1,0:T(8,128)(2,1)}, bf16[512,768]{1,0:T(8,128)(2,1)}, f32[128,768]{1,0:T(8,128)}, f32[512,768]{1,0:T(8,128)}, f32[48,1152]{1,0:T...) custom-call(f32[24,128]{1,0:T(8,128)} %get-tuple-element.102.refs_0_, ...), custom_call_target="tpu_custom_call" | custom-call | tf_op jit(solution)/shard_map/pallas_call | solution.py:1163

commit v2 on v1

--- a/solution.py
+++ b/solution.py
@@ -867,7 +867,6 @@
     tile_range(per, {2: both(("diag", 1), ("diag", 2))})
     red.core(3)
     red.core(4)
-    red.far(0)
     red.near(1)
     wait("hid", "ga_a", "ga_b")
 
@@ -885,6 +884,7 @@
         copy.start()
     load("proj", r_proj, gpj)
     red.near(2)
+    red.far(0)
     red.diag(3)
     red.diag(4)
     for copy in outs:

time: 222 us -> 222 us (level)
  no operation moved by 1% of the time
where the time goes in v2:
time: 222 us
  Pallas kernels  220 us (99%)
    pallas_call x1, Pallas kernels, forward(): pl.pallas_call(functools.partial(forward_kernel, shape, widths), out_shap...  109 us
    pallas_call x1, Pallas kernels, backward(): pl.pallas_call(functools.partial(backward_kernel, shape, widths), out_sha...  106 us
    pallas_call x1, Pallas kernels, finish(): pl.pallas_call(functools.partial(finish_kernel, spans), out_shape=[S(a.sh...  4.92 us

profile of v2, /device:TPU:0, one launch (start us, length us, event | category | flops | bytes accessed | tf_op | source)
XLA Modules:
  0.0 221.9 jit_solution(13504495563030071839)
XLA Ops:
  0.7 1.4 pad_add_fusion.refs_0_
  2.1 109.1 %shard_map.365 = (bf16[768,2304]{1,0:T(8,128)(2,1)}, bf16[768,768]{1,0:T(8,128)(2,1)}, bf16[768,3072]{1,0:T(8,128)(2,1)}, bf16[768,3072]{1,0:T(8,128)(2,1)}, bf1...) custom-call(bf16[32,128]{1,0:T(8,128)(2,1)} %pad_add_fusion.refs_0_,, ...), custom_call_target="tpu_custom_call" | custom-call | tf_op jit(solution)/shard_map/pallas_call | solution.py:566
  111.2 105.6 %shard_map.366 = (bf16[128,768]{1,0:T(8,128)(2,1)}, bf16[512,768]{1,0:T(8,128)(2,1)}, f32[128,768]{1,0:T(8,128)}, f32[512,768]{1,0:T(8,128)}, f32[48,1152]{1,0:T...) custom-call(bf16[3072,768]{1,0:T(8,128)(2,1)} %get-tuple-element.76., ...), custom_call_target="tpu_custom_call" | custom-call | tf_op jit(solution)/shard_map/pallas_call | solution.py:1122
  216.8 4.9 %shard_map.367 = (bf16[128,768]{1,0:T(8,128)(2,1)}, bf16[512,768]{1,0:T(8,128)(2,1)}, f32[128,768]{1,0:T(8,128)}, f32[512,768]{1,0:T(8,128)}, f32[48,1152]{1,0:T...) custom-call(f32[24,128]{1,0:T(8,128)} %get-tuple-element.102.refs_0_, ...), custom_call_target="tpu_custom_call" | custom-call | tf_op jit(solution)/shard_map/pallas_call | solution.py:1163
